TPU v7x, 128 devices: a whole 4x4x4 slice. The times are simulated.
128 devices in a mesh: layer: 2 (over core), row: 64 (over z, y, x).
Axes of the slice: x: 4, y: 4, z: 4, core: 2. Of those that a mesh axis runs over, the one named last changes fastest.
Arguments:
- sources: bfloat16 [2, 4608, 512], P('layer', 'row'), may hold values from -2 to 2
- green_down: bfloat16 [2, 4608, 4608], P('layer', 'row')
- green_up: bfloat16 [2, 4608, 4608], P('layer', 'row')
- material: int32 [8, 4608], P('layer', 'row'), may hold values 0 or 1
- pml_cells: int32 [1], replicated, may hold values from 4 to 39
Outputs:
- residual: bfloat16 [8, 4608, 512], P('layer', 'row')
All inputs are finite; a program needn't handle non-finite values. No bound on the sum of `material` on one device may be relied on, other than what follows from the above.
Results may differ from a plain program's by a relative error of at most 0.005.
Values may be sent and summed in bfloat16 or wider, within the bound.
A program may use at most 64 MiB of HBM per device.

v0:
```python
import jax
import jax.numpy as jnp
from jax import lax
from jax.sharding import PartitionSpec as P

BS = 256


def shifted(value, axis, steps):
    count = lax.axis_size(axis)
    leading, last = (max(0, -steps), min(count, count - steps))
    return lax.ppermute(value, axis, [(source, source + steps) for source in range(leading, last)])


def side_by_side(arrays, axis, dim, along):
    ends, at = ([], 0)
    for a in arrays[:-1]:
        at += a.shape[along]
        ends.append(at)
    both = jnp.concatenate(arrays, axis=along)
    return tuple(jnp.split(lax.all_gather(both, axis, axis=dim, tiled=True), ends, axis=along))


def with_halo(value, sides, width):
    edges = {}
    for axis, dim in sides:
        devices, length = (lax.axis_size(axis), value.shape[dim])
        up = [(i, (i + 1) % devices) for i in range(devices - 1)]
        last = lax.slice_in_dim(value, length - width, length, axis=dim)
        leading = lax.slice_in_dim(value, 0, width, axis=dim)
        edges[dim] = (
            lax.ppermute(last, axis, up),
            lax.ppermute(leading, axis, [(b, a) for a, b in up]),
        )
    done = []
    for _, dim in sides:
        low, high = edges[dim]
        around = [(width, width) if d in done else (0, 0) for d in range(value.ndim)]
        value = jnp.concatenate([jnp.pad(low, around), value, jnp.pad(high, around)], axis=dim)
        done.append(dim)
    return value


def take_down(last):
    return shifted(last, "layer", 1)


def take_up(last):
    return shifted(last, "layer", -1)


def folder(matrix, active, total, piece):
    return lax.cond(
        active, lambda: jnp.dot(matrix, piece, preferred_element_type=jnp.float32), lambda: total
    )


def ramp(index, count, thick):
    dist = jnp.minimum(index, count - 1 - index).astype(jnp.float32)
    return jnp.maximum(thick - dist, 0.0) / thick


def local(sources, green_down, green_up, material, pml_cells):
    source = sources[0]
    down_matrix = green_down[0]
    up_matrix = green_up[0]
    rows, total = source.shape
    layers = lax.axis_size("layer")
    here = lax.axis_index("layer")
    batches = total // BS
    width = total // batches
    ticks = layers + batches - 1

    def store(buffer, result, active, start, size):
        old = lax.dynamic_slice_in_dim(buffer, start, size, 1)
        return lax.dynamic_update_slice_in_dim(buffer, jnp.where(active, result, old), start, 1)

    up_rank = layers - 1 - here
    empty = jnp.zeros((rows, width), jnp.float32)
    blank = jnp.zeros((rows, width), jnp.bfloat16)
    store_init = jnp.zeros((rows, total), jnp.bfloat16)

    def inputs(incoming, tick, rank):
        batch = tick - rank
        active = jnp.logical_and(batch >= 0, batch < batches)
        start = jnp.clip(batch, 0, batches - 1) * width
        piece = lax.dynamic_slice_in_dim(source, start, width, 1)
        entry = (piece.astype(jnp.float32) + incoming.astype(jnp.float32)).astype(jnp.bfloat16)
        return (entry, active, start)

    def both_step(tick, state):
        last_down, last_up, buffer_down, buffer_up = state
        entry_down, active_down, start_down = inputs(take_down(last_down), tick, here)
        entry_up, active_up, start_up = inputs(take_up(last_up), tick, up_rank)
        pieces = side_by_side((entry_down, entry_up), "row", 0, 1)
        sum_down = folder(down_matrix, active_down, empty, pieces[0])
        sum_up = folder(up_matrix, active_up, empty, pieces[1])
        result_down = sum_down.astype(jnp.bfloat16)
        result_up = sum_up.astype(jnp.bfloat16)
        return (
            result_down,
            result_up,
            store(buffer_down, result_down, active_down, start_down, width),
            store(buffer_up, result_up, active_up, start_up, width),
        )

    final = lax.fori_loop(0, ticks, both_step, (blank, blank, store_init, store_init))
    down = final[2]
    up = final[3]
    wave = source.astype(jnp.float32) + down.astype(jnp.float32) + up.astype(jnp.float32)
    planes = material.shape[0]
    factor = (planes - jnp.arange(planes, dtype=jnp.float32)) / planes
    slab = wave[None, :, :] * factor[:, None, None]
    thick = pml_cells[0].astype(jnp.float32)
    plane_index = here * planes + jnp.arange(planes, dtype=jnp.int32)
    point_index = lax.axis_index("row") * rows + jnp.arange(rows, dtype=jnp.int32)
    ramp_z = ramp(plane_index, layers * planes, thick)
    ramp_m = ramp(point_index, rows * lax.axis_size("row"), thick)
    sigma = 3.0 * (ramp_z[:, None] * ramp_z[:, None] + ramp_m[None, :] * ramp_m[None, :])
    kappa = 1.0 + 1.5 * material.astype(jnp.float32)
    padded = with_halo(slab.astype(jnp.bfloat16), (("layer", 0), ("row", 1)), 1).astype(slab.dtype)
    beside = padded[2:, 1:-1] + padded[:-2, 1:-1] + padded[1:-1, 2:] + padded[1:-1, :-2]
    result = kappa[:, :, None] * ((4.0 + sigma)[:, :, None] * slab - beside)
    return result.astype(jnp.bfloat16)


def solution(mesh):
    return jax.shard_map(
        local,
        mesh=mesh,
        in_specs=(
            P("layer", "row", None),
            P("layer", "row", None),
            P("layer", "row", None),
            P("layer", "row"),
            P(),
        ),
        out_specs=P("layer", "row", None),
        check_vma=False,
    )
```

profile of v0, /device:TPU:1, one launch (start us, length us, event | category | flops | bytes accessed | tf_op | source)
XLA Modules:
  0.0 269.2 jit_solution(15884839280318397296)
XLA Ops:
  7.8 240.8 %while.19 = (s32[]{:T(128)}, bf16[72,256]{1,0:T(8,128)(2,1)}, bf16[72,256]{1,0:T(8,128)(2,1)}, bf16[72,512]{1,0:T(8,128)(2,1)S(1)}, bf16[72,512]{1,0:T(8,128)(2,...) while((s32[]{:T(128)}, bf16[72,256]{1,0:T(8,128)(2,1)}, ...), condition=%wide.region_5.6_spmd, body=%wide.region_0.5_spmd.sunk | while | flops 340107264 | bytes 21381664 | solution.py:107
  7.8 1.4 collective-permute-start
  9.2 3.3 %collective-permute-start.1 = (bf16[72,256]{1,0:T(8,128)(2,1)}, bf16[72,256]{1,0:T(8,128)(2,1)S(1)}, u32[]{:S(2)}, u32[]{:S(2)}) collective-permute-start(bf16[72,256]{1,0:T(8,128)(2,1)} %get-tuple-element.323), channel_id=1, source_target_pairs={{64,0},{65,1},{66,2},{67,3},{68,4},{69,5},{70,6},{71,7},{72,8},{73... | collective-permute-start | bytes 110600 | tf_op jit(solution)/shard_map/while/body/eval_jaxpr/ppermute | solution.py:12
  12.6 1.0 collective-permute-done.1
  13.6 0.9 add_convert_fusion.3
  15.2 70.8 %all-gather.2.cloned.1.call-done = bf16[4608,512]{1,0:T(8,128)(2,1)} async-done(((bf16[72,512]{1,0:T(8,128)(2,1)}), bf16[4608,512]{1,0:T(8,128)(2,1)}) %all-gather.2.cloned.1.call-update) | async-done | bytes 4718608 | tf_op jit(solution)/shard_map/while/body/eval_jaxpr/all_gather | solution.py:21
  86.0 3.0 %conditional.5 = (bf16[72,256]{1,0:T(8,128)(2,1)}) conditional(s32[]{:T(128)} %convert_element_type.169, () %tuple.59, (bf16[4608,512]{1,0:T(8,128)(2,1)}, bf16[72,4608]{1,0:T(8,128)(2,1)}) %tuple.60), branch_computations={%region_3.3_spmd, %region_4.4_spmd} | conditional | flops 169887744 | bytes 3059720 | solution.py:53
  86.0 3.0 %fusion.7 = bf16[72,256]{1,0:T(8,128)(2,1)} fusion(bf16[72,4608]{1,0:T(8,128)(2,1)} %get-tuple-element.190, bf16[4608,512]{1,0:T(8,128)(2,1)} %get-tuple-element.191), kind=kOutput, calls=%fused_computation.5 | convolution fusion | flops 169887744 | bytes 3059712 | tf_op jit(solution)/shard_map/while/body/eval_jaxpr/cond/branch_1_fun/dot_general | solution.py:54
  90.5 1.3 collective-permute-start
  91.8 4.2 %collective-permute-start.1 = (bf16[72,256]{1,0:T(8,128)(2,1)}, bf16[72,256]{1,0:T(8,128)(2,1)S(1)}, u32[]{:S(2)}, u32[]{:S(2)}) collective-permute-start(bf16[72,256]{1,0:T(8,128)(2,1)} %get-tuple-element.323), channel_id=1, source_target_pairs={{64,0},{65,1},{66,2},{67,3},{68,4},{69,5},{70,6},{71,7},{72,8},{73... | collective-permute-start | bytes 110600 | tf_op jit(solution)/shard_map/while/body/eval_jaxpr/ppermute | solution.py:12
  96.0 1.0 collective-permute-done.1
  97.1 0.8 add_convert_fusion.3
  98.6 65.2 %all-gather.2.cloned.1.call-done = bf16[4608,512]{1,0:T(8,128)(2,1)} async-done(((bf16[72,512]{1,0:T(8,128)(2,1)}), bf16[4608,512]{1,0:T(8,128)(2,1)}) %all-gather.2.cloned.1.call-update) | async-done | bytes 4718608 | tf_op jit(solution)/shard_map/while/body/eval_jaxpr/all_gather | solution.py:21
  163.8 3.0 %conditional.5 = (bf16[72,256]{1,0:T(8,128)(2,1)}) conditional(s32[]{:T(128)} %convert_element_type.169, () %tuple.59, (bf16[4608,512]{1,0:T(8,128)(2,1)}, bf16[72,4608]{1,0:T(8,128)(2,1)}) %tuple.60), branch_computations={%region_3.3_spmd, %region_4.4_spmd} | conditional | flops 169887744 | bytes 3059720 | solution.py:53
  163.8 3.0 %fusion.7 = bf16[72,256]{1,0:T(8,128)(2,1)} fusion(bf16[72,4608]{1,0:T(8,128)(2,1)} %get-tuple-element.190, bf16[4608,512]{1,0:T(8,128)(2,1)} %get-tuple-element.191), kind=kOutput, calls=%fused_computation.5 | convolution fusion | flops 169887744 | bytes 3059712 | tf_op jit(solution)/shard_map/while/body/eval_jaxpr/cond/branch_1_fun/dot_general | solution.py:54
  166.8 3.0 %conditional.4 = (bf16[72,256]{1,0:T(8,128)(2,1)}) conditional(s32[]{:T(128)} %convert_element_type.168, () %tuple.57, (bf16[4608,512]{1,0:T(8,128)(2,1)}, bf16[72,4608]{1,0:T(8,128)(2,1)}) %tuple.58), branch_computations={%region_1.1_spmd, %region_2.2_spmd} | conditional | flops 169887744 | bytes 3059720 | solution.py:53
  166.8 3.0 %fusion.2 = bf16[72,256]{1,0:T(8,128)(2,1)} fusion(bf16[72,4608]{1,0:T(8,128)(2,1)} %get-tuple-element.188, bf16[4608,512]{1,0:T(8,128)(2,1)} %get-tuple-element.189), kind=kOutput, calls=%fused_computation.2 | convolution fusion | flops 169887744 | bytes 3059712 | tf_op jit(solution)/shard_map/while/body/eval_jaxpr/cond/branch_1_fun/dot_general | solution.py:54
  169.9 0.8 select_dynamic-update-slice_fusion.3
  170.7 1.3 collective-permute-start
  172.0 4.2 %collective-permute-start.1 = (bf16[72,256]{1,0:T(8,128)(2,1)}, bf16[72,256]{1,0:T(8,128)(2,1)S(1)}, u32[]{:S(2)}, u32[]{:S(2)}) collective-permute-start(bf16[72,256]{1,0:T(8,128)(2,1)} %get-tuple-element.323), channel_id=1, source_target_pairs={{64,0},{65,1},{66,2},{67,3},{68,4},{69,5},{70,6},{71,7},{72,8},{73... | collective-permute-start | bytes 110600 | tf_op jit(solution)/shard_map/while/body/eval_jaxpr/ppermute | solution.py:12
  176.3 1.0 collective-permute-done.1
  177.3 0.9 add_convert_fusion.3
  178.9 65.2 %all-gather.2.cloned.1.call-done = bf16[4608,512]{1,0:T(8,128)(2,1)} async-done(((bf16[72,512]{1,0:T(8,128)(2,1)}), bf16[4608,512]{1,0:T(8,128)(2,1)}) %all-gather.2.cloned.1.call-update) | async-done | bytes 4718608 | tf_op jit(solution)/shard_map/while/body/eval_jaxpr/all_gather | solution.py:21
  244.7 3.0 %conditional.4 = (bf16[72,256]{1,0:T(8,128)(2,1)}) conditional(s32[]{:T(128)} %convert_element_type.168, () %tuple.57, (bf16[4608,512]{1,0:T(8,128)(2,1)}, bf16[72,4608]{1,0:T(8,128)(2,1)}) %tuple.58), branch_computations={%region_1.1_spmd, %region_2.2_spmd} | conditional | flops 169887744 | bytes 3059720 | solution.py:53
  244.7 3.0 %fusion.2 = bf16[72,256]{1,0:T(8,128)(2,1)} fusion(bf16[72,4608]{1,0:T(8,128)(2,1)} %get-tuple-element.188, bf16[4608,512]{1,0:T(8,128)(2,1)} %get-tuple-element.189), kind=kOutput, calls=%fused_computation.2 | convolution fusion | flops 169887744 | bytes 3059712 | tf_op jit(solution)/shard_map/while/body/eval_jaxpr/cond/branch_1_fun/dot_general | solution.py:54
  248.6 0.9 convert_add_fusion
  249.6 1.3 collective-permute-start.3
  250.9 4.2 %collective-permute-start.4 = (bf16[1,72,512]{2,1,0:T(8,128)(2,1)S(1)}, bf16[1,72,512]{2,1,0:T(8,128)(2,1)S(1)}, u32[]{:S(2)}, u32[]{:S(2)}) collective-permute-start(bf16[1,72,512]{2,1,0:T(8,128)(2,1)S(1)} %get-tuple-element.232), channel_id=1, source_target_pairs={{64,0},{65,1},{66,2},{67,3},{68,4},{69,5},{70,6},{71,7},{72,8},{73... | collective-permute-start | bytes 221192 | tf_op jit(solution)/shard_map/ppermute | solution.py:33
  255.2 1.9 collective-permute-start.2
  257.1 1.3 collective-permute-start.5
  259.2 2.3 collective-permute-done.5
  261.7 1.0 fusion.14
  (35 shorter events, 7.8 us)
Async XLA Ops:
  7.8 251.3 %copy-start = (s32[4,72]{1,0:T(4,128)S(1)}, s32[4,72]{1,0:T(4,128)}, u32[]{:S(2)}) copy-start(s32[4,72]{1,0:T(4,128)} %param.14) | copy-start | bytes 3460
  7.8 78.2 %all-gather.2.cloned.1.call-start = ((), (), s32[]{:S(2)}) async-start(), calls=%async_computation | async-start | bytes 4792320 | tf_op jit(solution)/shard_map/while/body/eval_jaxpr/all_gather | solution.py:21
  7.8 4.8 %collective-permute-start = (bf16[72,256]{1,0:T(8,128)(2,1)}, bf16[72,256]{1,0:T(8,128)(2,1)S(1)}, u32[]{:S(2)}, u32[]{:S(2)}) collective-permute-start(bf16[72,256]{1,0:T(8,128)(2,1)} %get-tuple-element.322), channel_id=1, source_target_pairs={{0,64},{1,65},{2,66},{3,67},{4,68},{5,69},{6,70},{7,71},{8,72},{9,... | collective-permute-start | bytes 110600 | tf_op jit(solution)/shard_map/while/body/eval_jaxpr/ppermute | solution.py:12
  9.2 4.4 %collective-permute-start.1 = (bf16[72,256]{1,0:T(8,128)(2,1)}, bf16[72,256]{1,0:T(8,128)(2,1)S(1)}, u32[]{:S(2)}, u32[]{:S(2)}) collective-permute-start(bf16[72,256]{1,0:T(8,128)(2,1)} %get-tuple-element.323), channel_id=1, source_target_pairs={{64,0},{65,1},{66,2},{67,3},{68,4},{69,5},{70,6},{71,7},{72,8},{73... | collective-permute-start | bytes 110600 | tf_op jit(solution)/shard_map/while/body/eval_jaxpr/ppermute | solution.py:12
  90.4 73.4 %all-gather.2.cloned.1.call-start = ((), (), s32[]{:S(2)}) async-start(), calls=%async_computation | async-start | bytes 4792320 | tf_op jit(solution)/shard_map/while/body/eval_jaxpr/all_gather | solution.py:21
  90.5 5.6 %collective-permute-start = (bf16[72,256]{1,0:T(8,128)(2,1)}, bf16[72,256]{1,0:T(8,128)(2,1)S(1)}, u32[]{:S(2)}, u32[]{:S(2)}) collective-permute-start(bf16[72,256]{1,0:T(8,128)(2,1)} %get-tuple-element.322), channel_id=1, source_target_pairs={{0,64},{1,65},{2,66},{3,67},{4,68},{5,69},{6,70},{7,71},{8,72},{9,... | collective-permute-start | bytes 110600 | tf_op jit(solution)/shard_map/while/body/eval_jaxpr/ppermute | solution.py:12
  91.8 5.3 %collective-permute-start.1 = (bf16[72,256]{1,0:T(8,128)(2,1)}, bf16[72,256]{1,0:T(8,128)(2,1)S(1)}, u32[]{:S(2)}, u32[]{:S(2)}) collective-permute-start(bf16[72,256]{1,0:T(8,128)(2,1)} %get-tuple-element.323), channel_id=1, source_target_pairs={{64,0},{65,1},{66,2},{67,3},{68,4},{69,5},{70,6},{71,7},{72,8},{73... | collective-permute-start | bytes 110600 | tf_op jit(solution)/shard_map/while/body/eval_jaxpr/ppermute | solution.py:12
  170.7 73.4 %all-gather.2.cloned.1.call-start = ((), (), s32[]{:S(2)}) async-start(), calls=%async_computation | async-start | bytes 4792320 | tf_op jit(solution)/shard_map/while/body/eval_jaxpr/all_gather | solution.py:21
  170.7 5.6 %collective-permute-start = (bf16[72,256]{1,0:T(8,128)(2,1)}, bf16[72,256]{1,0:T(8,128)(2,1)S(1)}, u32[]{:S(2)}, u32[]{:S(2)}) collective-permute-start(bf16[72,256]{1,0:T(8,128)(2,1)} %get-tuple-element.322), channel_id=1, source_target_pairs={{0,64},{1,65},{2,66},{3,67},{4,68},{5,69},{6,70},{7,71},{8,72},{9,... | collective-permute-start | bytes 110600 | tf_op jit(solution)/shard_map/while/body/eval_jaxpr/ppermute | solution.py:12
  172.0 5.3 %collective-permute-start.1 = (bf16[72,256]{1,0:T(8,128)(2,1)}, bf16[72,256]{1,0:T(8,128)(2,1)S(1)}, u32[]{:S(2)}, u32[]{:S(2)}) collective-permute-start(bf16[72,256]{1,0:T(8,128)(2,1)} %get-tuple-element.323), channel_id=1, source_target_pairs={{64,0},{65,1},{66,2},{67,3},{68,4},{69,5},{70,6},{71,7},{72,8},{73... | collective-permute-start | bytes 110600 | tf_op jit(solution)/shard_map/while/body/eval_jaxpr/ppermute | solution.py:12
  249.6 11.9 %collective-permute-start.3 = (bf16[1,72,512]{2,1,0:T(8,128)(2,1)S(1)}, bf16[1,72,512]{2,1,0:T(8,128)(2,1)S(1)}, u32[]{:S(2)}, u32[]{:S(2)}) collective-permute-start(bf16[1,72,512]{2,1,0:T(8,128)(2,1)S(1)} %get-tuple-element.231), channel_id=1, source_target_pairs={{0,64},{1,65},{2,66},{3,67},{4,68},{5,69},{6,70},{7,71},{8,72},{9,... | collective-permute-start | bytes 221192 | tf_op jit(solution)/shard_map/ppermute | solution.py:32
  250.9 10.6 %collective-permute-start.4 = (bf16[1,72,512]{2,1,0:T(8,128)(2,1)S(1)}, bf16[1,72,512]{2,1,0:T(8,128)(2,1)S(1)}, u32[]{:S(2)}, u32[]{:S(2)}) collective-permute-start(bf16[1,72,512]{2,1,0:T(8,128)(2,1)S(1)} %get-tuple-element.232), channel_id=1, source_target_pairs={{64,0},{65,1},{66,2},{67,3},{68,4},{69,5},{70,6},{71,7},{72,8},{73... | collective-permute-start | bytes 221192 | tf_op jit(solution)/shard_map/ppermute | solution.py:33
  255.2 4.0 %collective-permute-start.2 = (bf16[4,1,512]{2,1,0:T(2,128)(2,1)S(1)}, bf16[4,1,512]{2,1,0:T(2,128)(2,1)S(1)}, u32[]{:S(2)}, u32[]{:S(2)}) collective-permute-start(bf16[4,1,512]{2,1,0:T(2,128)(2,1)S(1)} %get-tuple-element.233), channel_id=1, source_target_pairs={{0,1},{1,2},{2,3},{3,4},{4,5},{5,6},{6,7},{7,8},{8,9},{9,10},{10,1... | collective-permute-start | bytes 12296 | tf_op jit(solution)/shard_map/ppermute | solution.py:32
  257.1 4.4 %collective-permute-start.5 = (bf16[4,1,512]{2,1,0:T(2,128)(2,1)S(1)}, bf16[4,1,512]{2,1,0:T(2,128)(2,1)S(1)}, u32[]{:S(2)}, u32[]{:S(2)}) collective-permute-start(bf16[4,1,512]{2,1,0:T(2,128)(2,1)S(1)} %get-tuple-element.234), channel_id=1, source_target_pairs={{1,0},{2,1},{3,2},{4,3},{5,4},{6,5},{7,6},{8,7},{9,8},{10,9},{11,1... | collective-permute-start | bytes 12296 | tf_op jit(solution)/shard_map/ppermute | solution.py:33
Sparse Core Ops, SparseCore 0:
  15.3 70.6 all-gather.1
  98.7 65.0 all-gather.1
  179.0 65.0 all-gather.1
where the time goes:
time: 273 us; the launch traced here: 269 us
  waiting for transfers between devices  207 us (76%)
  starting transfers between devices  24.6 us (9%)
  between operations  13.8 us (5%)
  matrix products  12.1 us (4%)
  other arithmetic  9.13 us (3%)
    all_gather x3, waiting for transfers between devices, side_by_side(): lax.all_gather(both, axis, axis=dim, tiled=True)  201 us
    ppermute x6, starting transfers between devices, shifted(): lax.ppermute(value, axis, [(source, source + steps) for source in range(l...  15.8 us
    dot_general x4, matrix products, folder(): jnp.dot(matrix, piece, preferred_element_type=jnp.float32)  12.1 us
    ppermute x2, starting transfers between devices, with_halo(): lax.ppermute(leading, axis, [(b, a) for a, b in up])  5.53 us
  transfers between devices with their start and end apart: 13, of which 7 were waited for; matrix products, arithmetic and copies ran while one was open for 0% of the time, Pallas kernels for 0%

commit v1 on v0

v1 whole, which is shorter than its diff:
```python
import functools

import jax
import jax.numpy as jnp
from jax import lax
from jax.experimental import pallas as pl
from jax.experimental.pallas import tpu as pltpu
from jax.sharding import PartitionSpec as P

MESH = pl.DeviceIdType.MESH
F32, BF16 = jnp.float32, jnp.bfloat16
N = 4
LANES = 128


def device(layer, z, y, x):
    return (layer, (z * N + y) * N + x)


def kernel(
    src, gd, gu, mat, pml, out,
    green, xin, res, fin, hal, own88, other, wave, kc, kf, mt,
    bulk_s, bulk_r, fwd_s, fwd_r, src_s, src_r, x_s, x_r, fin_s, fin_r,
    hal_s, hal_r, edge_s, edge_r, loc,
):
    layer = lax.axis_index("layer")
    row = lax.axis_index("row")
    z, y, x = row // (N * N), (row // N) % N, row % N
    group = z * N + y
    rows = src.shape[1]
    chunk = N * N * rows
    sweep = x // 2
    sib = 1 - layer
    mine = (layer + sweep) % 2

    def shift(a, d):
        return lax.rem(a + d, N)

    def remote(s, d, ss, rs, to):
        return pltpu.make_async_remote_copy(
            src_ref=s, dst_ref=d, send_sem=ss, recv_sem=rs, device_id=to, device_id_type=MESH
        )

    greet = [device(sib, z, y, x)]
    for d in (1, 2, 3):
        greet += [device(layer, z, y, shift(x, d)), device(sib, z, y, shift(x, d))]
        greet += [device(layer, z, shift(y, d), x), device(layer, shift(z, d), y, x)]
    barrier = pltpu.get_barrier_semaphore()
    for to in greet:
        pl.semaphore_signal(barrier, inc=1, device_id=to, device_id_type=MESH)

    def part_of_source(to_x, to_layer):
        quarter = 2 * lax.rem(to_x, 2) + to_layer
        return src.at[0, :, pl.ds(pl.multiple_of(quarter * LANES, LANES), LANES)]

    own_src = pltpu.make_async_copy(part_of_source(x, layer), xin.at[mine, z, y, x], loc.at[0])
    own_src.start()
    own_88 = pltpu.make_async_copy(src.at[0], own88.at[pl.ds(8, rows)], loc.at[1])
    own_88.start()
    own_green = []
    for c in range(N):
        cols = pl.ds(pl.multiple_of(shift(z, c) * chunk, LANES), chunk)
        to = green.at[mine, shift(z, c), x]
        for s, ref in ((0, gd), (1, gu)):
            @pl.when(sweep == s)
            def _(ref=ref, cols=cols, to=to, c=c):
                pltpu.make_async_copy(ref.at[0, :, cols], to, loc.at[2 + c]).start()
        own_green.append(pltpu.make_async_copy(gd.at[0, :, cols], to, loc.at[2 + c]))

    pl.semaphore_wait(barrier, len(greet))

    def source_copy(dx, dl):
        to_x = shift(x, dx)
        to_l = layer if dl == 0 else sib
        rnd = (layer + to_x // 2) % 2
        return remote(
            part_of_source(to_x, to_l), xin.at[rnd, z, y, x], src_s.at[dl, dx], src_r.at[dl, dx],
            device(to_l, z, y, to_x),
        )

    pairs = [(dx, dl) for dx in (2, 1, 3, 0) for dl in (0, 1) if (dx, dl) != (0, 0)]
    source_copies = {p: source_copy(*p) for p in pairs}
    for p in pairs:
        source_copies[p].start()

    def green_copy(dx, c, ref, s):
        cols = pl.ds(pl.multiple_of(shift(z, c) * chunk, LANES), chunk)
        rnd = (layer + s) % 2
        return remote(
            ref.at[0, :, cols], green.at[rnd, shift(z, c), x], bulk_s.at[dx, c], bulk_r.at[dx, c],
            device(layer, z, y, shift(x, dx)),
        )

    order = (0, 1, 3, 2)
    for first in (True, False):
        for s, ref in ((0, gd), (1, gu)):
            now = (layer == s) if first else (layer != s)
            for dx in (2, 1, 3):
                @pl.when(jnp.logical_and(now, shift(x, dx) // 2 == s))
                def _(s=s, ref=ref, dx=dx):
                    for c in order:
                        green_copy(dx, c, ref, s).start()

    other_copy = remote(src.at[0], other, edge_s.at[2], edge_r.at[2], device(sib, z, y, x))
    other_copy.start()

    rows_at = lax.broadcasted_iota(jnp.int32, (rows, LANES), 0) + row * rows
    thick = jnp.full((rows, LANES), pml[0].astype(F32))
    total = rows * N * N * N

    def ramp(index, count):
        dist = jnp.minimum(index, count - 1 - index).astype(F32)
        return jnp.maximum(thick - dist, 0.0) / thick

    ramp_m = ramp(rows_at, total)
    mt[...] = jnp.zeros_like(mt)
    mt[0:4, 0:rows] = 1.0 + 1.5 * mat[...].astype(F32)
    kappa = mt[...].T
    for k in range(4):
        ramp_z = ramp(jnp.full((rows, LANES), layer * 4 + k, jnp.int32), 8)
        sigma = 3.0 * (ramp_z * ramp_z + ramp_m * ramp_m)
        f = (4 - k) / 4
        around = (0 if k == 0 else (5 - k) / 4) + (0 if k == 3 else (3 - k) / 4)
        kap = jnp.broadcast_to(kappa[0:rows, k : k + 1], (rows, LANES))
        kc[k] = kap * (f * (4.0 + sigma) - around)
        kf[k] = kap * f
    res[:, 0:8] = jnp.zeros((2, 8, LANES), BF16)
    res[:, 4 * rows + 8 :] = jnp.zeros((2, 8, LANES), BF16)

    halves = (pl.ds(0, 2), pl.ds(2, 2))

    def plane_copy(rnd, part, from_z, from_y, sz, sy, to_z, to_y):
        at = xin.at[rnd, from_z, from_y, halves[part]]
        return remote(
            at, at, x_s.at[rnd, part, sz, sy], x_r.at[rnd, part, sz, sy],
            device(layer, to_z, to_y, x),
        )

    def first_stage(rnd):
        done = []
        for d in (2, 1, 3):
            done.append(plane_copy(rnd, 0, z, y, 0, d, z, shift(y, d)))
            done.append(plane_copy(rnd, 1, z, y, d, 0, shift(z, d), y))
        for d in (2, 1, 3):
            done.append(plane_copy(rnd, 0, z, y, d, 0, shift(z, d), y))
            done.append(plane_copy(rnd, 1, z, y, 0, d, z, shift(y, d)))
        for c in done:
            c.start()
        return done

    def arrival(rnd, part, sz, sy):
        from_z, from_y = shift(z, N - sz), shift(y, N - sy)
        at = xin.at[rnd, from_z, from_y, halves[part]]
        return remote(
            at, at, x_s.at[rnd, part, sz, sy], x_r.at[rnd, part, sz, sy], device(layer, z, y, x)
        )

    def second_stage(rnd):
        done = []
        for d in (1, 3, 2):
            arrival(rnd, 0, 0, d).wait_recv()
            for q in (2, 1, 3):
                done.append(plane_copy(rnd, 0, z, shift(y, N - d), q, d, shift(z, q), y))
                done[-1].start()
            arrival(rnd, 1, d, 0).wait_recv()
            for q in (2, 1, 3):
                done.append(plane_copy(rnd, 1, shift(z, N - d), y, d, q, z, shift(y, q)))
                done[-1].start()
        return done

    def wait_plane(rnd, sz):
        for sy in (0, 1, 3, 2):
            for part in (0, 1):
                if (sz, sy) != (0, 0) and not (part == 0 and sz == 0) and not (part == 1 and sy == 0):
                    arrival(rnd, part, sz, sy).wait_recv()

    def forward(dx, c):
        at = green.at[mine, shift(z, c), shift(x, N - dx)]
        return remote(at, at, fwd_s.at[dx, c], fwd_r.at[dx, c], device(sib, z, y, x))

    def from_sibling(dx, c):
        at = green.at[1 - mine, shift(z, c), shift(x, N - dx)]
        return remote(at, at, fwd_s.at[dx, c], fwd_r.at[dx, c], device(sib, z, y, x))

    def wait_green(rnd, c):
        @pl.when(mine == rnd)
        def _():
            for dx in (0, 1, 3, 2):
                if dx == 0:
                    own_green[c].wait()
                else:
                    green_copy(dx, c, gd, 0).wait_recv()
                forward(dx, c).start()

        @pl.when(mine != rnd)
        def _():
            for dx in (0, 1, 3, 2):
                from_sibling(dx, c).wait_recv()

    def product(rnd):
        acc = None
        for c in order:
            wait_green(rnd, c)
            wait_plane(rnd, (N - c) % N)
            g = green[rnd, shift(z, c)].reshape(N * rows, chunk)
            v = xin[rnd, shift(z, c)].reshape(chunk, LANES)
            term = jnp.dot(g, v, preferred_element_type=F32)
            acc = term if acc is None else acc + term
        return acc.astype(BF16)

    def share(rnd):
        at_layer = sweep if rnd == 0 else 1 - sweep
        quarter = 2 * lax.rem(x, 2) + layer
        done = []
        for dx in (2, 1, 3, 0):
            to_x = shift(x, dx)
            at = res.at[rnd, pl.ds(pl.multiple_of(to_x * rows, 8), rows + 16)]
            to = fin.at[sweep, at_layer, quarter]
            for dl in (0, 1):
                if (dx, dl) == (0, 0):
                    done.append(pltpu.make_async_copy(at, to, loc.at[6 + rnd]))
                else:
                    done.append(remote(
                        at, to, fin_s.at[rnd, dl, dx], fin_r.at[rnd, dl, dx],
                        device(layer if dl == 0 else sib, z, y, to_x),
                    ))
        to = hal.at[sweep, quarter]
        up = remote(
            res.at[rnd, pl.ds(N * rows, 8)], to, hal_s.at[rnd, 0], hal_r.at[x, layer],
            (at_layer, lax.rem((group + 1) * N, N * N * N)),
        )
        down = remote(
            res.at[rnd, pl.ds(8, 8)], to, hal_s.at[rnd, 1], hal_r.at[x, layer],
            (at_layer, lax.rem(group * N + N * N * N - 1, N * N * N)),
        )
        return done, up, down

    def start_share(shared):
        done, up, down = shared

        @pl.when(group < N * N - 1)
        def _():
            up.start()

        @pl.when(group > 0)
        def _():
            down.start()

        for c in done:
            c.start()

    def sent_share(shared):
        done, up, down = shared

        @pl.when(group < N * N - 1)
        def _():
            up.wait_send()

        @pl.when(group > 0)
        def _():
            down.wait_send()

        for c in done[:-2] + done[-1:]:
            c.wait_send()

    own_src.wait()
    for p in pairs:
        source_copies[p].wait_recv()
    sent = first_stage(0)
    sent += second_stage(0)
    res[0, 8 : N * rows + 8] = product(0)

    entry = xin[1, z, y].reshape(N * rows, LANES).astype(F32) + res[0, 8 : N * rows + 8].astype(F32)
    xin[1, z, y] = entry.astype(BF16).reshape(N, rows, LANES)
    sent2 = first_stage(1)
    shared = share(0)
    start_share(shared)

    own_88.wait()
    edge_up = remote(
        src.at[0, pl.ds(rows - 8, 8)], own88.at[pl.ds(0, 8)], edge_s.at[0], edge_r.at[0],
        (layer, lax.rem(row + 1, N * N * N)),
    )
    edge_down = remote(
        src.at[0, pl.ds(0, 8)], own88.at[pl.ds(rows + 8, 8)], edge_s.at[1], edge_r.at[1],
        (layer, lax.rem(row + N * N * N - 1, N * N * N)),
    )
    last = N * N * N - 1

    @pl.when(row < last)
    def _():
        edge_up.start()

    @pl.when(row > 0)
    def _():
        edge_down.start()

    sent2 += second_stage(1)
    for c in sent:
        c.wait_send()
    for p in pairs:
        source_copies[p].wait_send()
    other_copy.wait()

    @pl.when(row < last)
    def _():
        edge_up.wait_send()
        edge_down.wait_recv()

    @pl.when(row > 0)
    def _():
        edge_down.wait_send()
        edge_up.wait_recv()

    sent_share(shared)
    res[1, 8 : N * rows + 8] = product(1)
    shared2 = share(1)
    start_share(shared2)
    for c in sent2:
        c.wait_send()
    for dx in (1, 2, 3):
        for c in range(N):
            green_copy(dx, c, gd, 0).wait_send()
    for dx in range(N):
        for c in range(N):
            forward(dx, c).wait_send()

    sent_share(shared2)

    for done, _, _ in (shared, shared2):
        done[-2].wait()
        for c in done[:-2] + done[-1:]:
            c.wait_recv()

    def wait_halo():
        for a in range(N):
            for b in range(2):
                remote(
                    res.at[0, pl.ds(0, 8)], hal.at[0, 0], hal_s.at[0, 0], hal_r.at[a, b],
                    device(sib, z, y, x),
                ).wait_recv()

    for q in range(4):
        cols = slice(q * LANES, (q + 1) * LANES)
        wave[:, cols] = (
            own88[:, cols].astype(F32) + fin[0, layer, q].astype(F32) + fin[1, layer, q].astype(F32)
        )

    def edge(at):
        wait_halo()
        for q in range(4):
            cols = slice(q * LANES, (q + 1) * LANES)
            wave[at : at + 8, cols] = (
                own88[at : at + 8, cols].astype(F32) + hal[0, q].astype(F32) + hal[1, q].astype(F32)
            )

    @pl.when(jnp.logical_and(x == 0, group > 0))
    def _():
        edge(0)

    @pl.when(jnp.logical_and(x == N - 1, group < N * N - 1))
    def _():
        edge(rows + 8)

    @pl.when(row == 0)
    def _():
        wave[0:8] = jnp.zeros((8, wave.shape[1]), F32)

    @pl.when(row == last)
    def _():
        wave[rows + 8 :] = jnp.zeros((8, wave.shape[1]), F32)

    here = layer.astype(F32)
    for q in range(4):
        cols = slice(q * LANES, (q + 1) * LANES)
        a = wave[8 : rows + 8, cols]
        b = wave[7 : rows + 7, cols] + wave[9 : rows + 9, cols]
        o = (
            other[:, cols].astype(F32)
            + fin[0, sib, q, 8 : rows + 8].astype(F32)
            + fin[1, sib, q, 8 : rows + 8].astype(F32)
        )
        for k in range(4):
            value = kc[k] * a - kf[k] * b
            if k == 0:
                value = value - kf[k] * (o * (0.25 * here))
            if k == 3:
                value = value - kf[k] * (o * (4.0 * (1.0 - here)))
            out[k, :, cols] = value.astype(BF16)


def local(source, green_down, green_up, material, pml_cells):
    rows, columns = source.shape[1:]
    points = green_down.shape[2]
    dma = pltpu.SemaphoreType.DMA
    hbm, vmem = pl.BlockSpec(memory_space=pl.ANY), pl.BlockSpec(memory_space=pltpu.VMEM)
    return pl.pallas_call(
        kernel,
        out_shape=jax.ShapeDtypeStruct((4, rows, columns), BF16),
        in_specs=[hbm, hbm, hbm, vmem, pl.BlockSpec(memory_space=pltpu.SMEM)],
        out_specs=vmem,
        scratch_shapes=[
            pltpu.VMEM((2, N, N, rows, points // N), BF16),
            pltpu.VMEM((2, N, N, N, rows, LANES), BF16),
            pltpu.VMEM((2, N * rows + 16, LANES), BF16),
            pltpu.VMEM((2, 2, 4, rows + 16, LANES), BF16),
            pltpu.VMEM((2, 4, 8, LANES), BF16),
            pltpu.VMEM((rows + 16, columns), BF16),
            pltpu.VMEM((rows, columns), BF16),
            pltpu.VMEM((rows + 16, columns), F32),
            pltpu.VMEM((4, rows, LANES), F32),
            pltpu.VMEM((4, rows, LANES), F32),
            pltpu.VMEM((8, LANES), F32),
            dma((N, N)), dma((N, N)), dma((N, N)), dma((N, N)),
            dma((2, N)), dma((2, N)),
            dma((2, 2, N, N)), dma((2, 2, N, N)),
            dma((2, 2, N)), dma((2, 2, N)),
            dma((2, 2)), dma((N, 2)),
            dma((3,)), dma((3,)),
            dma((8,)),
        ],
        compiler_params=pltpu.CompilerParams(
            collective_id=0, has_side_effects=True, vmem_limit_bytes=48 << 20
        ),
    )(source, green_down, green_up, material, pml_cells)


def solution(mesh):
    return jax.shard_map(
        local,
        mesh=mesh,
        in_specs=(
            P("layer", "row", None),
            P("layer", "row", None),
            P("layer", "row", None),
            P("layer", "row"),
            P(),
        ),
        out_specs=P("layer", "row", None),
        check_vma=False,
    )
```

time: 273 us -> 65.7 us (0.24); the launches traced: 269 us -> 65.5 us
  waiting for transfers between devices: 207 us -> 0 us
  Pallas kernels: 0 us -> 60.4 us
  starting transfers between devices: 24.6 us -> 0 us
  between operations: 13.8 us -> 0.67 us
  matrix products: 12.1 us -> 0 us
  other arithmetic: 9.13 us -> 0 us
    all_gather x3 -> x0, waiting for transfers between devices: 201 us -> none  [side_by_side(): lax.all_gather(both, axis, axis=dim, tiled=True)]
    pallas_call x0 -> x1, Pallas kernels: none -> 60.4 us  [local(): pl.pallas_call(kernel, out_shape=jax.ShapeDtypeStruct((4, rows, columns),...]
    ppermute x10 -> x0, starting transfers between devices: 24.5 us -> none  [the longest x6 15.8 us: shifted(): lax.ppermute(value, axis, [(source, source + steps) for source in range(l...]
    dot_general x4 -> x0, matrix products: 12.1 us -> none  [folder(): jnp.dot(matrix, piece, preferred_element_type=jnp.float32)]
    ppermute x10 -> x0, waiting for transfers between devices: 5.4 us -> none  [the longest x6 3.07 us: shifted(): lax.ppermute(value, axis, [(source, source + steps) for source in range(l...]
    unnamed x2 -> x9, local copies, waits for them, and re-layouts: 0.01 us -> 4.45 us
    convert_element_type x6 -> x0, other arithmetic: 3.8 us -> none  [the longest x3 2.54 us: inputs(): (piece.astype(jnp.float32) + incoming.astype(jnp.float32)).astype(jnp.bfl...]
  transfers between devices with their start and end apart: 13 -> 0, of which waited for: 7 -> 0; matrix products, arithmetic and copies ran while one was open for 0% -> 0% of each run, Pallas kernels for 0% -> 0%
where the time goes in v1:
time: 65.7 us; the launch traced here: 65.5 us
  Pallas kernels  60.4 us (92%)
  local copies, waits for them, and re-layouts  4.45 us (7%)
  between operations  0.67 us (1%)
    pallas_call x1, Pallas kernels, local(): pl.pallas_call(kernel, out_shape=jax.ShapeDtypeStruct((4, rows, columns),...  60.4 us
    unnamed x9, local copies, waits for them, and re-layouts  4.45 us

profile of v1, /device:TPU:1, one launch (start us, length us, event | category | flops | bytes accessed | tf_op | source)
XLA Modules:
  0.0 65.5 jit_solution(11167610409692031068)
XLA Ops:
  0.7 0.0 copy-start
  0.7 1.1 %copy-done = bf16[1,72,4608]{2,1,0:T(8,128)(2,1)S(1)} copy-done((bf16[1,72,4608]{2,1,0:T(8,128)(2,1)S(1)}, bf16[1,72,4608]{2,1,0:T(8,128)(2,1)}, u32[]{:S(2)}) %copy-start) | copy-done | bytes 663576
  1.7 0.0 copy-start.1
  1.7 1.1 %copy-done.1 = bf16[1,72,4608]{2,1,0:T(8,128)(2,1)S(1)} copy-done((bf16[1,72,4608]{2,1,0:T(8,128)(2,1)S(1)}, bf16[1,72,4608]{2,1,0:T(8,128)(2,1)}, u32[]{:S(2)}) %copy-start.1) | copy-done | bytes 663576
  2.8 0.0 copy-start.2
  2.8 0.9 %copy-done.2 = bf16[1,72,512]{2,1,0:T(8,128)(2,1)S(1)} copy-done((bf16[1,72,512]{2,1,0:T(8,128)(2,1)S(1)}, bf16[1,72,512]{2,1,0:T(8,128)(2,1)}, u32[]{:S(2)}) %copy-start.2) | copy-done | bytes 73752
  3.7 0.0 copy-start.3
  3.7 0.7 %copy-done.3 = s32[4,72]{1,0:T(4,128)S(1)} copy-done((s32[4,72]{1,0:T(4,128)S(1)}, s32[4,72]{1,0:T(4,128)}, u32[]{:S(2)}) %copy-start.3) | copy-done | bytes 1176
  4.4 60.4 %shard_map.55 = bf16[4,72,512]{2,1,0:T(8,128)(2,1)S(1)} custom-call(bf16[1,72,512]{2,1,0:T(8,128)(2,1)S(1)} %copy-done.2, bf16[1,72,4608]{2,1,0:T(8,128)(2,1)S(1)} %copy-done, bf16[1,72,4608]{2,1,0:T(8,128)(2,1)S(1)} %copy-done.1, s32[4,72]{1,0:T(4,128)S(1)} %copy-done.3, s32[1]{0:T(128)S(6)} %copy.7.pml), custom_call_target="tpu_custom_call" | custom-call | tf_op jit(solution)/shard_map/pallas_call | solution.py:397
  64.8 0.7 %copy.8 = bf16[4,72,512]{2,1,0:T(8,128)(2,1)} copy(bf16[4,72,512]{2,1,0:T(8,128)(2,1)S(1)} %shard_map.55) | data formatting | bytes 589824
Async XLA Ops:
  0.7 1.1 %copy-start = (bf16[1,72,4608]{2,1,0:T(8,128)(2,1)S(1)}, bf16[1,72,4608]{2,1,0:T(8,128)(2,1)}, u32[]{:S(2)}) copy-start(bf16[1,72,4608]{2,1,0:T(8,128)(2,1)} %gd.1) | copy-start | bytes 1990660
  1.7 1.1 %copy-start.1 = (bf16[1,72,4608]{2,1,0:T(8,128)(2,1)S(1)}, bf16[1,72,4608]{2,1,0:T(8,128)(2,1)}, u32[]{:S(2)}) copy-start(bf16[1,72,4608]{2,1,0:T(8,128)(2,1)} %gu.1) | copy-start | bytes 1990660
  2.8 0.9 %copy-start.2 = (bf16[1,72,512]{2,1,0:T(8,128)(2,1)S(1)}, bf16[1,72,512]{2,1,0:T(8,128)(2,1)}, u32[]{:S(2)}) copy-start(bf16[1,72,512]{2,1,0:T(8,128)(2,1)} %src.1) | copy-start | bytes 221188
  3.7 0.7 %copy-start.3 = (s32[4,72]{1,0:T(4,128)S(1)}, s32[4,72]{1,0:T(4,128)}, u32[]{:S(2)}) copy-start(s32[4,72]{1,0:T(4,128)} %mat.1) | copy-start | bytes 3460

commit v2 on v1

--- a/solution.py
+++ b/solution.py
@@ -49,6 +49,9 @@
     for to in greet:
         pl.semaphore_signal(barrier, inc=1, device_id=to, device_id_type=MESH)
 
+    def green_part(ref, c):
+        return ref.at[0, :, pl.ds(pl.multiple_of(shift(z, c) * chunk, LANES), chunk)]
+
     def part_of_source(to_x, to_layer):
         quarter = 2 * lax.rem(to_x, 2) + to_layer
         return src.at[0, :, pl.ds(pl.multiple_of(quarter * LANES, LANES), LANES)]
@@ -59,13 +62,12 @@
     own_88.start()
     own_green = []
     for c in range(N):
-        cols = pl.ds(pl.multiple_of(shift(z, c) * chunk, LANES), chunk)
         to = green.at[mine, shift(z, c), x]
         for s, ref in ((0, gd), (1, gu)):
             @pl.when(sweep == s)
-            def _(ref=ref, cols=cols, to=to, c=c):
-                pltpu.make_async_copy(ref.at[0, :, cols], to, loc.at[2 + c]).start()
-        own_green.append(pltpu.make_async_copy(gd.at[0, :, cols], to, loc.at[2 + c]))
+            def _(ref=ref, to=to, c=c):
+                pltpu.make_async_copy(green_part(ref, c), to, loc.at[2 + c]).start()
+        own_green.append(pltpu.make_async_copy(green_part(gd, c), to, loc.at[2 + c]))
 
     pl.semaphore_wait(barrier, len(greet))
 
@@ -83,23 +85,64 @@
     for p in pairs:
         source_copies[p].start()
 
-    def green_copy(dx, c, ref, s):
-        cols = pl.ds(pl.multiple_of(shift(z, c) * chunk, LANES), chunk)
-        rnd = (layer + s) % 2
-        return remote(
-            ref.at[0, :, cols], green.at[rnd, shift(z, c), x], bulk_s.at[dx, c], bulk_r.at[dx, c],
-            device(layer, z, y, shift(x, dx)),
-        )
-
+    mate = x + 1 - 2 * (x % 2)
+    outer = lax.rem(x + N - 1 + 2 * (x % 2), N)
+    far = shift(x, 2)
+    OWN, MATE, OUTER, FAR = range(4)
+    place = {OWN: x, MATE: mate, OUTER: outer, FAR: far}
     order = (0, 1, 3, 2)
-    for first in (True, False):
+
+    def to_mate(c, ref):
+        return remote(
+            green_part(ref, c), green.at[mine, shift(z, c), x],
+            bulk_s.at[MATE, c], bulk_r.at[MATE, c], device(layer, z, y, mate),
+        )
+
+    def to_outer(c, ref):
+        return remote(
+            green_part(ref, c), green.at[1 - mine, shift(z, c), x],
+            bulk_s.at[OUTER, c], bulk_r.at[OUTER, c], device(layer, z, y, outer),
+        )
+
+    def far_to_mate(c):
+        at = green.at[mine, shift(z, c), outer]
+        return remote(at, at, bulk_s.at[FAR, c], bulk_r.at[FAR, c], device(layer, z, y, mate))
+
+    def to_sibling(kind, c, ref=None):
+        at = green.at[mine, shift(z, c), place[kind]]
+        return remote(
+            at if ref is None else green_part(ref, c), at, fwd_s.at[kind, c], fwd_r.at[kind, c],
+            device(sib, z, y, x),
+        )
+
+    def send_own(refs, other):
+        for s, ref in ((0, refs[0]), (1, refs[1])):
+            @pl.when(sweep == s)
+            def _(ref=ref):
+                for c in order:
+                    (to_outer if other else to_mate)(c, ref).start()
+
+    def own_to_sibling():
         for s, ref in ((0, gd), (1, gu)):
-            now = (layer == s) if first else (layer != s)
-            for dx in (2, 1, 3):
-                @pl.when(jnp.logical_and(now, shift(x, dx) // 2 == s))
-                def _(s=s, ref=ref, dx=dx):
-                    for c in order:
-                        green_copy(dx, c, ref, s).start()
+            @pl.when(sweep == s)
+            def _(ref=ref):
+                for c in order:
+                    to_sibling(OWN, c, ref).start()
+
+    def relay(c):
+        to_outer(c, gd).wait_recv()
+        far_to_mate(c).start()
+        to_sibling(OUTER, c).start()
+
+    @pl.when(mine == 0)
+    def _():
+        send_own((gd, gu), False)
+
+    @pl.when(mine == 1)
+    def _():
+        send_own((gu, gd), True)
+
+    own_to_sibling()
 
     other_copy = remote(src.at[0], other, edge_s.at[2], edge_r.at[2], device(sib, z, y, x))
     other_copy.start()
@@ -158,6 +201,10 @@
     def second_stage(rnd):
         done = []
         for d in (1, 3, 2):
+            if rnd == 0:
+                @pl.when(mine == 0)
+                def _(d=d):
+                    relay(order[(0, 0, 2, 1)[d]])
             arrival(rnd, 0, 0, d).wait_recv()
             for q in (2, 1, 3):
                 done.append(plane_copy(rnd, 0, z, shift(y, N - d), q, d, shift(z, q), y))
@@ -174,28 +221,19 @@
                 if (sz, sy) != (0, 0) and not (part == 0 and sz == 0) and not (part == 1 and sy == 0):
                     arrival(rnd, part, sz, sy).wait_recv()
 
-    def forward(dx, c):
-        at = green.at[mine, shift(z, c), shift(x, N - dx)]
-        return remote(at, at, fwd_s.at[dx, c], fwd_r.at[dx, c], device(sib, z, y, x))
-
-    def from_sibling(dx, c):
-        at = green.at[1 - mine, shift(z, c), shift(x, N - dx)]
-        return remote(at, at, fwd_s.at[dx, c], fwd_r.at[dx, c], device(sib, z, y, x))
-
     def wait_green(rnd, c):
         @pl.when(mine == rnd)
         def _():
-            for dx in (0, 1, 3, 2):
-                if dx == 0:
-                    own_green[c].wait()
-                else:
-                    green_copy(dx, c, gd, 0).wait_recv()
-                forward(dx, c).start()
+            to_mate(c, gd).wait_recv()
+            to_sibling(MATE, c).start()
+            far_to_mate(c).wait_recv()
+            to_sibling(FAR, c).start()
+            own_green[c].wait()
 
         @pl.when(mine != rnd)
         def _():
-            for dx in (0, 1, 3, 2):
-                from_sibling(dx, c).wait_recv()
+            for kind in (OWN, OUTER, MATE, FAR):
+                to_sibling(kind, c).wait_recv()
 
     def product(rnd):
         acc = None
@@ -268,6 +306,16 @@
         source_copies[p].wait_recv()
     sent = first_stage(0)
     sent += second_stage(0)
+
+    @pl.when(mine == 0)
+    def _():
+        relay(order[3])
+        send_own((gu, gd), True)
+
+    @pl.when(mine == 1)
+    def _():
+        send_own((gd, gu), False)
+
     res[0, 8 : N * rows + 8] = product(0)
 
     entry = xin[1, z, y].reshape(N * rows, LANES).astype(F32) + res[0, 8 : N * rows + 8].astype(F32)
@@ -295,8 +343,18 @@
     def _():
         edge_down.start()
 
+
+    @pl.when(mine == 1)
+    def _():
+        for c in order:
+            relay(c)
+
     sent2 += second_stage(1)
-    for c in sent:
+    res[1, 8 : N * rows + 8] = product(1)
+    shared2 = share(1)
+    start_share(shared2)
+
+    for c in sent + sent2:
         c.wait_send()
     for p in pairs:
         source_copies[p].wait_send()
@@ -313,18 +371,12 @@
         edge_up.wait_recv()
 
     sent_share(shared)
-    res[1, 8 : N * rows + 8] = product(1)
-    shared2 = share(1)
-    start_share(shared2)
-    for c in sent2:
-        c.wait_send()
-    for dx in (1, 2, 3):
-        for c in range(N):
-            green_copy(dx, c, gd, 0).wait_send()
-    for dx in range(N):
-        for c in range(N):
-            forward(dx, c).wait_send()
-
+    for c in range(N):
+        to_mate(c, gd).wait_send()
+        to_outer(c, gd).wait_send()
+        far_to_mate(c).wait_send()
+        for kind in range(4):
+            to_sibling(kind, c).wait_send()
     sent_share(shared2)
 
     for done, _, _ in (shared, shared2):
@@ -393,7 +445,7 @@
     rows, columns = source.shape[1:]
     points = green_down.shape[2]
     dma = pltpu.SemaphoreType.DMA
-    hbm, vmem = pl.BlockSpec(memory_space=pl.ANY), pl.BlockSpec(memory_space=pltpu.VMEM)
+    hbm, vmem = pl.BlockSpec(memory_space=pltpu.HBM), pl.BlockSpec(memory_space=pltpu.VMEM)
     return pl.pallas_call(
         kernel,
         out_shape=jax.ShapeDtypeStruct((4, rows, columns), BF16),
@@ -420,7 +472,7 @@
             dma((8,)),
         ],
         compiler_params=pltpu.CompilerParams(
-            collective_id=0, has_side_effects=True, vmem_limit_bytes=48 << 20
+            collective_id=0, has_side_effects=True, vmem_limit_bytes=60 << 20
         ),
     )(source, green_down, green_up, material, pml_cells)
 

time: 65.7 us -> 57.5 us (0.88)
  Pallas kernels: 60.4 us -> 55 us
  local copies, waits for them, and re-layouts: 4.45 us -> 1.69 us
    pallas_call x1, Pallas kernels: 60.4 us -> 55 us  [local(): pl.pallas_call(kernel, out_shape=jax.ShapeDtypeStruct((4, rows, columns),...]
    unnamed x9 -> x1, local copies, waits for them, and re-layouts: 4.45 us -> 1.69 us
where the time goes in v2:
time: 57.5 us; the launch traced here: 57.4 us
  Pallas kernels  55 us (96%)
  local copies, waits for them, and re-layouts  1.69 us (3%)
  between operations  0.66 us (1%)
    pallas_call x1, Pallas kernels, local(): pl.pallas_call(kernel, out_shape=jax.ShapeDtypeStruct((4, rows, columns),...  55 us
    unnamed x1, local copies, waits for them, and re-layouts  1.69 us

profile of v2, /device:TPU:1, one launch (start us, length us, event | category | flops | bytes accessed | tf_op | source)
XLA Modules:
  0.0 57.4 jit_solution(6528341102356001839)
XLA Ops:
  0.7 55.0 %shard_map.55 = bf16[4,72,512]{2,1,0:T(8,128)(2,1)} custom-call(bf16[1,72,512]{2,1,0:T(8,128)(2,1)} %src.1, bf16[1,72,4608]{2,1,0:T(8,128)(2,1)} %gd.1, bf16[1,72,4608]{2,1,0:T(8,128)(2,1)} %gu.1, s32[4,72]{1,0:T(4,128)} %mat.1, s32[1]{0:T(128)S(6)} %copy.7.pml), custom_call_target="tpu_custom_call" | custom-call | tf_op jit(solution)/shard_map/pallas_call | solution.py:449
  55.7 1.7 %copy.8 = bf16[4,72,512]{2,1,0:T(8,128)(2,1)} copy(bf16[4,72,512]{2,1,0:T(8,128)(2,1)} %shard_map.55) | data formatting | bytes 589824

commit v3 on v2

--- a/solution.py
+++ b/solution.py
@@ -19,7 +19,7 @@
 
 def kernel(
     src, gd, gu, mat, pml, out,
-    green, xin, res, fin, hal, own88, other, wave, kc, kf, mt,
+    pml_s, mat_v, green, xin, res, fin, hal, own88, other, wave, kc, kf, mt,
     bulk_s, bulk_r, fwd_s, fwd_r, src_s, src_r, x_s, x_r, fin_s, fin_r,
     hal_s, hal_r, edge_s, edge_r, loc,
 ):
@@ -52,13 +52,20 @@
     def green_part(ref, c):
         return ref.at[0, :, pl.ds(pl.multiple_of(shift(z, c) * chunk, LANES), chunk)]
 
-    def part_of_source(to_x, to_layer):
-        quarter = 2 * lax.rem(to_x, 2) + to_layer
-        return src.at[0, :, pl.ds(pl.multiple_of(quarter * LANES, LANES), LANES)]
-
-    own_src = pltpu.make_async_copy(part_of_source(x, layer), xin.at[mine, z, y, x], loc.at[0])
+    own_rows = own88.at[pl.ds(8, rows)]
+
+    def quarter_of(to_x, to_layer):
+        return pl.ds(pl.multiple_of((2 * lax.rem(to_x, 2) + to_layer) * LANES, LANES), LANES)
+
+    pml_copy = pltpu.make_async_copy(pml, pml_s, loc.at[8])
+    pml_copy.start()
+    mat_copy = pltpu.make_async_copy(mat, mat_v, loc.at[9])
+    mat_copy.start()
+    own_src = pltpu.make_async_copy(
+        src.at[0, :, quarter_of(x, layer)], xin.at[mine, z, y, x], loc.at[0]
+    )
     own_src.start()
-    own_88 = pltpu.make_async_copy(src.at[0], own88.at[pl.ds(8, rows)], loc.at[1])
+    own_88 = pltpu.make_async_copy(src.at[0], own_rows, loc.at[1])
     own_88.start()
     own_green = []
     for c in range(N):
@@ -69,6 +76,7 @@
                 pltpu.make_async_copy(green_part(ref, c), to, loc.at[2 + c]).start()
         own_green.append(pltpu.make_async_copy(green_part(gd, c), to, loc.at[2 + c]))
 
+    own_88.wait()
     pl.semaphore_wait(barrier, len(greet))
 
     def source_copy(dx, dl):
@@ -76,7 +84,7 @@
         to_l = layer if dl == 0 else sib
         rnd = (layer + to_x // 2) % 2
         return remote(
-            part_of_source(to_x, to_l), xin.at[rnd, z, y, x], src_s.at[dl, dx], src_r.at[dl, dx],
+            own88.at[pl.ds(8, rows), quarter_of(to_x, to_l)], xin.at[rnd, z, y, x], src_s.at[dl, dx], src_r.at[dl, dx],
             device(to_l, z, y, to_x),
         )
 
@@ -144,11 +152,13 @@
 
     own_to_sibling()
 
-    other_copy = remote(src.at[0], other, edge_s.at[2], edge_r.at[2], device(sib, z, y, x))
+    other_copy = remote(own_rows, other, edge_s.at[2], edge_r.at[2], device(sib, z, y, x))
     other_copy.start()
 
+    pml_copy.wait()
+    mat_copy.wait()
     rows_at = lax.broadcasted_iota(jnp.int32, (rows, LANES), 0) + row * rows
-    thick = jnp.full((rows, LANES), pml[0].astype(F32))
+    thick = jnp.full((rows, LANES), pml_s[0].astype(F32))
     total = rows * N * N * N
 
     def ramp(index, count):
@@ -157,7 +167,7 @@
 
     ramp_m = ramp(rows_at, total)
     mt[...] = jnp.zeros_like(mt)
-    mt[0:4, 0:rows] = 1.0 + 1.5 * mat[...].astype(F32)
+    mt[0:4, 0:rows] = 1.0 + 1.5 * mat_v[...].astype(F32)
     kappa = mt[...].T
     for k in range(4):
         ramp_z = ramp(jnp.full((rows, LANES), layer * 4 + k, jnp.int32), 8)
@@ -239,6 +249,10 @@
         acc = None
         for c in order:
             wait_green(rnd, c)
+            if rnd == 0 and c == order[1]:
+                @pl.when(mine == 1)
+                def _():
+                    send_own((gd, gu), False)
             wait_plane(rnd, (N - c) % N)
             g = green[rnd, shift(z, c)].reshape(N * rows, chunk)
             v = xin[rnd, shift(z, c)].reshape(chunk, LANES)
@@ -301,9 +315,17 @@
         for c in done[:-2] + done[-1:]:
             c.wait_send()
 
-    own_src.wait()
-    for p in pairs:
-        source_copies[p].wait_recv()
+    def wait_sources(same_core):
+        if same_core:
+            own_src.wait()
+        for p in pairs:
+            if p[1] == (0 if same_core else 1):
+                source_copies[p].wait_recv()
+
+    for m in (0, 1):
+        @pl.when(mine == m)
+        def _(m=m):
+            wait_sources(m == 0)
     sent = first_stage(0)
     sent += second_stage(0)
 
@@ -312,25 +334,24 @@
         relay(order[3])
         send_own((gu, gd), True)
 
-    @pl.when(mine == 1)
-    def _():
-        send_own((gd, gu), False)
-
     res[0, 8 : N * rows + 8] = product(0)
 
+    for m in (0, 1):
+        @pl.when(mine == m)
+        def _(m=m):
+            wait_sources(m == 1)
     entry = xin[1, z, y].reshape(N * rows, LANES).astype(F32) + res[0, 8 : N * rows + 8].astype(F32)
     xin[1, z, y] = entry.astype(BF16).reshape(N, rows, LANES)
     sent2 = first_stage(1)
     shared = share(0)
     start_share(shared)
 
-    own_88.wait()
     edge_up = remote(
-        src.at[0, pl.ds(rows - 8, 8)], own88.at[pl.ds(0, 8)], edge_s.at[0], edge_r.at[0],
+        own88.at[pl.ds(rows, 8)], own88.at[pl.ds(0, 8)], edge_s.at[0], edge_r.at[0],
         (layer, lax.rem(row + 1, N * N * N)),
     )
     edge_down = remote(
-        src.at[0, pl.ds(0, 8)], own88.at[pl.ds(rows + 8, 8)], edge_s.at[1], edge_r.at[1],
+        own88.at[pl.ds(8, 8)], own88.at[pl.ds(rows + 8, 8)], edge_s.at[1], edge_r.at[1],
         (layer, lax.rem(row + N * N * N - 1, N * N * N)),
     )
     last = N * N * N - 1
@@ -449,9 +470,11 @@
     return pl.pallas_call(
         kernel,
         out_shape=jax.ShapeDtypeStruct((4, rows, columns), BF16),
-        in_specs=[hbm, hbm, hbm, vmem, pl.BlockSpec(memory_space=pltpu.SMEM)],
+        in_specs=[hbm] * 5,
         out_specs=vmem,
         scratch_shapes=[
+            pltpu.SMEM((1,), jnp.int32),
+            pltpu.VMEM((4, rows), jnp.int32),
             pltpu.VMEM((2, N, N, rows, points // N), BF16),
             pltpu.VMEM((2, N, N, N, rows, LANES), BF16),
             pltpu.VMEM((2, N * rows + 16, LANES), BF16),
@@ -469,7 +492,7 @@
             dma((2, 2, N)), dma((2, 2, N)),
             dma((2, 2)), dma((N, 2)),
             dma((3,)), dma((3,)),
-            dma((8,)),
+            dma((10,)),
         ],
         compiler_params=pltpu.CompilerParams(
             collective_id=0, has_side_effects=True, vmem_limit_bytes=60 << 20

time: 57.5 us -> 51.5 us (0.90)
  Pallas kernels: 55 us -> 49 us
    pallas_call x1, Pallas kernels: 55 us -> 49 us  [local(): pl.pallas_call(kernel, out_shape=jax.ShapeDtypeStruct((4, rows, columns),...]
where the time goes in v3:
time: 51.5 us; the launch traced here: 51.3 us
  Pallas kernels  49 us (95%)
  local copies, waits for them, and re-layouts  1.69 us (3%)
  between operations  0.66 us (1%)
    pallas_call x1, Pallas kernels, local(): pl.pallas_call(kernel, out_shape=jax.ShapeDtypeStruct((4, rows, columns),...  49 us
    unnamed x1, local copies, waits for them, and re-layouts  1.69 us

profile of v3, /device:TPU:1, one launch (start us, length us, event | category | flops | bytes accessed | tf_op | source)
XLA Modules:
  0.0 51.3 jit_solution(2741582902422143526)
XLA Ops:
  0.7 49.0 %shard_map.55 = bf16[4,72,512]{2,1,0:T(8,128)(2,1)} custom-call(bf16[1,72,512]{2,1,0:T(8,128)(2,1)} %src.1, bf16[1,72,4608]{2,1,0:T(8,128)(2,1)} %gd.1, bf16[1,72,4608]{2,1,0:T(8,128)(2,1)} %gu.1, s32[4,72]{1,0:T(4,128)} %mat.1, s32[1]{0:T(128)S(6)} %copy.7.pml), custom_call_target="tpu_custom_call" | custom-call | tf_op jit(solution)/shard_map/pallas_call | solution.py:470
  49.6 1.7 %copy.8 = bf16[4,72,512]{2,1,0:T(8,128)(2,1)} copy(bf16[4,72,512]{2,1,0:T(8,128)(2,1)} %shard_map.55) | data formatting | bytes 589824

commit v4 on v3

--- a/solution.py
+++ b/solution.py
@@ -158,7 +158,7 @@
     pml_copy.wait()
     mat_copy.wait()
     rows_at = lax.broadcasted_iota(jnp.int32, (rows, LANES), 0) + row * rows
-    thick = jnp.full((rows, LANES), pml_s[0].astype(F32))
+    thick = jnp.full((rows, LANES), pml_s[0, 0].astype(F32))
     total = rows * N * N * N
 
     def ramp(index, count):
@@ -467,13 +467,17 @@
     points = green_down.shape[2]
     dma = pltpu.SemaphoreType.DMA
     hbm, vmem = pl.BlockSpec(memory_space=pltpu.HBM), pl.BlockSpec(memory_space=pltpu.VMEM)
+    held = [
+        pltpu.with_memory_space_constraint(v, pltpu.HBM)
+        for v in (source, green_down, green_up, material)
+    ]
     return pl.pallas_call(
         kernel,
         out_shape=jax.ShapeDtypeStruct((4, rows, columns), BF16),
         in_specs=[hbm] * 5,
         out_specs=vmem,
         scratch_shapes=[
-            pltpu.SMEM((1,), jnp.int32),
+            pltpu.SMEM((1, 1), jnp.int32),
             pltpu.VMEM((4, rows), jnp.int32),
             pltpu.VMEM((2, N, N, rows, points // N), BF16),
             pltpu.VMEM((2, N, N, N, rows, LANES), BF16),
@@ -495,9 +499,9 @@
             dma((10,)),
         ],
         compiler_params=pltpu.CompilerParams(
-            collective_id=0, has_side_effects=True, vmem_limit_bytes=60 << 20
+            collective_id=0, has_side_effects=True, vmem_limit_bytes=48 << 20
         ),
-    )(source, green_down, green_up, material, pml_cells)
+    )(*held, pml_cells.reshape(1, 1))
 
 
 def solution(mesh):

time: 51.5 us -> 49.8 us (0.967)
  local copies, waits for them, and re-layouts: 1.69 us -> 0.72 us
  Pallas kernels: 49 us -> 48.2 us
    unnamed x1, local copies, waits for them, and re-layouts: 1.69 us -> 0.72 us
    pallas_call x1, Pallas kernels: 49 us -> 48.2 us  [local(): pl.pallas_call(kernel, out_shape=jax.ShapeDtypeStruct((4, rows, columns),...]
where the time goes in v4:
time: 49.8 us; the launch traced here: 49.6 us
  Pallas kernels  48.2 us (97%)
  local copies, waits for them, and re-layouts  0.72 us (1%)
  between operations  0.66 us (1%)
    pallas_call x1, Pallas kernels, local(): pl.pallas_call(kernel, out_shape=jax.ShapeDtypeStruct((4, rows, columns),...  48.2 us

profile of v4, /device:TPU:1, one launch (start us, length us, event | category | flops | bytes accessed | tf_op | source)
XLA Modules:
  0.0 49.6 jit_solution(3505546560839005901)
XLA Ops:
  0.7 48.2 %shard_map.55 = bf16[4,72,512]{2,1,0:T(8,128)(2,1)S(1)} custom-call(bf16[1,72,512]{2,1,0:T(8,128)(2,1)} %src.1, bf16[1,72,4608]{2,1,0:T(8,128)(2,1)} %gd.1, bf16[1,72,4608]{2,1,0:T(8,128)(2,1)} %gu.1, s32[4,72]{1,0:T(4,128)} %mat.1, s32[1,1]{1,0:T(1,128)} %bitcast.1.pml), custom_call_target="tpu_custom_call" | custom-call | tf_op jit(solution)/shard_map/pallas_call | solution.py:474
  48.9 0.7 %copy.8 = bf16[4,72,512]{2,1,0:T(8,128)(2,1)} copy(bf16[4,72,512]{2,1,0:T(8,128)(2,1)S(1)} %shard_map.55) | data formatting | bytes 589824

commit v5 on v4

--- a/solution.py
+++ b/solution.py
@@ -344,7 +344,6 @@
     xin[1, z, y] = entry.astype(BF16).reshape(N, rows, LANES)
     sent2 = first_stage(1)
     shared = share(0)
-    start_share(shared)
 
     edge_up = remote(
         own88.at[pl.ds(rows, 8)], own88.at[pl.ds(0, 8)], edge_s.at[0], edge_r.at[0],
@@ -371,15 +370,18 @@
             relay(c)
 
     sent2 += second_stage(1)
-    res[1, 8 : N * rows + 8] = product(1)
-    shared2 = share(1)
-    start_share(shared2)
-
-    for c in sent + sent2:
+    start_share(shared)
+    for c in sent:
         c.wait_send()
     for p in pairs:
         source_copies[p].wait_send()
     other_copy.wait()
+    res[1, 8 : N * rows + 8] = product(1)
+    shared2 = share(1)
+    start_share(shared2)
+
+    for c in sent2:
+        c.wait_send()
 
     @pl.when(row < last)
     def _():

time: 49.8 us -> 48.9 us (0.982)
  Pallas kernels: 48.2 us -> 47.4 us
    pallas_call x1, Pallas kernels: 48.2 us -> 47.4 us  [local(): pl.pallas_call(kernel, out_shape=jax.ShapeDtypeStruct((4, rows, columns),...]
where the time goes in v5:
time: 48.9 us; the launch traced here: 48.8 us
  Pallas kernels  47.4 us (97%)
  local copies, waits for them, and re-layouts  0.72 us (1%)
  between operations  0.66 us (1%)
    pallas_call x1, Pallas kernels, local(): pl.pallas_call(kernel, out_shape=jax.ShapeDtypeStruct((4, rows, columns),...  47.4 us

profile of v5, /device:TPU:1, one launch (start us, length us, event | category | flops | bytes accessed | tf_op | source)
XLA Modules:
  0.0 48.8 jit_solution(8281951267948806361)
XLA Ops:
  0.7 47.4 %shard_map.55 = bf16[4,72,512]{2,1,0:T(8,128)(2,1)S(1)} custom-call(bf16[1,72,512]{2,1,0:T(8,128)(2,1)} %src.1, bf16[1,72,4608]{2,1,0:T(8,128)(2,1)} %gd.1, bf16[1,72,4608]{2,1,0:T(8,128)(2,1)} %gu.1, s32[4,72]{1,0:T(4,128)} %mat.1, s32[1,1]{1,0:T(1,128)} %bitcast.1.pml), custom_call_target="tpu_custom_call" | custom-call | tf_op jit(solution)/shard_map/pallas_call | solution.py:476
  48.1 0.7 %copy.8 = bf16[4,72,512]{2,1,0:T(8,128)(2,1)} copy(bf16[4,72,512]{2,1,0:T(8,128)(2,1)S(1)} %shard_map.55) | data formatting | bytes 589824

commit v6 on v5

--- a/solution.py
+++ b/solution.py
@@ -19,7 +19,7 @@
 
 def kernel(
     src, gd, gu, mat, pml, out,
-    pml_s, mat_v, green, xin, res, fin, hal, own88, other, wave, kc, kf, mt,
+    pml_s, mat_v, green, xin, res, fin, hal, own88, other, across, wave, kc, kf, mt,
     bulk_s, bulk_r, fwd_s, fwd_r, src_s, src_r, x_s, x_r, fin_s, fin_r,
     hal_s, hal_r, edge_s, edge_r, loc,
 ):
@@ -245,9 +245,11 @@
             for kind in (OWN, OUTER, MATE, FAR):
                 to_sibling(kind, c).wait_recv()
 
-    def product(rnd):
+    def product(rnd, idle=None):
         acc = None
         for c in order:
+            if idle is not None and c == order[3]:
+                idle()
             wait_green(rnd, c)
             if rnd == 0 and c == order[1]:
                 @pl.when(mine == 1)
@@ -376,12 +378,16 @@
     for p in pairs:
         source_copies[p].wait_send()
     other_copy.wait()
-    res[1, 8 : N * rows + 8] = product(1)
+    def sent_before():
+        for c in sent2:
+            c.wait_send()
+        for c in range(N):
+            to_outer(c, gd).wait_send()
+            to_sibling(OWN, c).wait_send()
+
+    res[1, 8 : N * rows + 8] = product(1, sent_before)
     shared2 = share(1)
     start_share(shared2)
-
-    for c in sent2:
-        c.wait_send()
 
     @pl.when(row < last)
     def _():
@@ -396,16 +402,22 @@
     sent_share(shared)
     for c in range(N):
         to_mate(c, gd).wait_send()
-        to_outer(c, gd).wait_send()
         far_to_mate(c).wait_send()
-        for kind in range(4):
+        for kind in (MATE, OUTER, FAR):
             to_sibling(kind, c).wait_send()
     sent_share(shared2)
 
-    for done, _, _ in (shared, shared2):
+    def wait_share(done):
         done[-2].wait()
         for c in done[:-2] + done[-1:]:
             c.wait_recv()
+
+    wait_share(shared[0])
+    for q in range(4):
+        cols = slice(q * LANES, (q + 1) * LANES)
+        wave[:, cols] = own88[:, cols].astype(F32) + fin[layer, layer, q].astype(F32)
+        across[:, cols] = other[:, cols].astype(F32) + fin[sib, sib, q, 8 : rows + 8].astype(F32)
+    wait_share(shared2[0])
 
     def wait_halo():
         for a in range(N):
@@ -417,9 +429,7 @@
 
     for q in range(4):
         cols = slice(q * LANES, (q + 1) * LANES)
-        wave[:, cols] = (
-            own88[:, cols].astype(F32) + fin[0, layer, q].astype(F32) + fin[1, layer, q].astype(F32)
-        )
+        wave[:, cols] = wave[:, cols] + fin[sib, layer, q].astype(F32)
 
     def edge(at):
         wait_halo()
@@ -450,11 +460,7 @@
         cols = slice(q * LANES, (q + 1) * LANES)
         a = wave[8 : rows + 8, cols]
         b = wave[7 : rows + 7, cols] + wave[9 : rows + 9, cols]
-        o = (
-            other[:, cols].astype(F32)
-            + fin[0, sib, q, 8 : rows + 8].astype(F32)
-            + fin[1, sib, q, 8 : rows + 8].astype(F32)
-        )
+        o = across[:, cols] + fin[layer, sib, q, 8 : rows + 8].astype(F32)
         for k in range(4):
             value = kc[k] * a - kf[k] * b
             if k == 0:
@@ -488,6 +494,7 @@
             pltpu.VMEM((2, 4, 8, LANES), BF16),
             pltpu.VMEM((rows + 16, columns), BF16),
             pltpu.VMEM((rows, columns), BF16),
+            pltpu.VMEM((rows, columns), F32),
             pltpu.VMEM((rows + 16, columns), F32),
             pltpu.VMEM((4, rows, LANES), F32),
             pltpu.VMEM((4, rows, LANES), F32),

time: 48.9 us -> 49 us (level)
  no operation moved by 1% of the time
where the time goes in v6:
time: 49 us; the launch traced here: 48.8 us
  Pallas kernels  47.4 us (97%)
  local copies, waits for them, and re-layouts  0.72 us (1%)
  between operations  0.66 us (1%)
    pallas_call x1, Pallas kernels, local(): pl.pallas_call(kernel, out_shape=jax.ShapeDtypeStruct((4, rows, columns),...  47.4 us

profile of v6, /device:TPU:1, one launch (start us, length us, event | category | flops | bytes accessed | tf_op | source)
XLA Modules:
  0.0 48.8 jit_solution(17142990312491675556)
XLA Ops:
  0.7 47.4 %shard_map.55 = bf16[4,72,512]{2,1,0:T(8,128)(2,1)S(1)} custom-call(bf16[1,72,512]{2,1,0:T(8,128)(2,1)} %src.1, bf16[1,72,4608]{2,1,0:T(8,128)(2,1)} %gd.1, bf16[1,72,4608]{2,1,0:T(8,128)(2,1)} %gu.1, s32[4,72]{1,0:T(4,128)} %mat.1, s32[1,1]{1,0:T(1,128)} %bitcast.1.pml), custom_call_target="tpu_custom_call" | custom-call | tf_op jit(solution)/shard_map/pallas_call | solution.py:482
  48.1 0.7 %copy.8 = bf16[4,72,512]{2,1,0:T(8,128)(2,1)} copy(bf16[4,72,512]{2,1,0:T(8,128)(2,1)S(1)} %shard_map.55) | data formatting | bytes 589824
